TPU v7x, 32 devices: a whole 2x2x4 slice. The times are simulated.
32 devices in a mesh: row: 4 (over z), col: 8 (over y, x, core).
Axes of the slice: x: 2, y: 2, z: 4, core: 2. Of those that a mesh axis runs over, the one named last changes fastest.
Arguments:
- hidden: bfloat16 [4096, 2048], P(('row', 'col')), may hold values from -6 to 6
- cached_lengths: int32 [4], replicated, may hold values from 1024 to 4096, as said below
- request_order: int32 [4], replicated, may hold values from 0 to 3, each once
- cache_keys: bfloat16 [4, 4096, 2048], P('row', None, 'col'), may hold values from -480 to 480
- cache_values: bfloat16 [4, 4096, 2048], P('row', None, 'col'), may hold values from -6 to 6
- attn_gain: bfloat16 [2048], replicated, may hold values from 0.5 to 1.5
- w_qkv: bfloat16 [2048, 16, 384], P(None, 'col'), may hold values from -0.125 to 0.125
- w_out: bfloat16 [2048, 2048], P('col'), may hold values from -0.125 to 0.125
- moe_gain: bfloat16 [2048], replicated, may hold values from 0.5 to 1.5
- expert_ids: int32 [4096, 6], P(('row', 'col')), may hold values from 0 to 63, all different within a row; in each aligned block of 128 rows (0 to 127, 128 to 255, ...) at most 16 rows name the same one
- gate_weights: bfloat16 [4096, 6], P(('row', 'col')), may hold values from 0.049804688 to 0.3984375
- w_in: bfloat16 [128, 2048, 1408], P(('row', 'col')), may hold values from -0.125 to 0.125
- w_down: bfloat16 [128, 704, 2048], P(('row', 'col')), may hold values from -0.15625 to 0.15625
Outputs:
- new_hidden: bfloat16 [4096, 2048], P(('row', 'col'))
- new_keys: bfloat16 [4096, 2048], P('row', 'col')
- new_values: bfloat16 [4096, 2048], P('row', 'col')
Inputs may be any that keep to these rules, and one draw needn't show every extreme that they name: `cached_lengths`: every request has at least a quarter of 4096 cached tokens, and some request has exactly 4096. `request_order`: each slot serves a different request. `expert_ids`: among the rows of one device (aligned blocks of 128 tokens) no expert is named by more than 16 rows, a bound that some block reaches.
All inputs are finite; a program needn't handle non-finite values.
Results may differ from a plain program's by a relative error of at most 0.015.
Values may be sent and summed in bfloat16 or wider, within the bound.
No kernel may reach another device: no remote copies, remote signals or barrier semaphores. Data moves between devices by JAX's collectives and lax.ppermute only.
A program may use at most 192 MiB of HBM per device.

v0:
```python
import jax
import jax.numpy as jnp
from jax import lax
from jax.sharding import PartitionSpec as P

EXPERTS = 64
WINDOW = 4096
SINKS = 4
CAP = 16
EPS = 1e-06
THETA = 10000.0


def rms_scale(matrix, scaling):
    values = matrix.astype(jnp.float32)
    factor = lax.rsqrt(jnp.mean(values * values, axis=-1, keepdims=True) + EPS)
    return values * factor * scaling.astype(jnp.float32)


def rotate(vectors, positions):
    half_width = vectors.shape[-1] // 2
    frequency = THETA ** (-2.0 * jnp.arange(half_width, dtype=jnp.float32) / vectors.shape[-1])
    angles = positions.astype(jnp.float32)[..., None] * frequency
    cosine = jnp.cos(angles)[..., None, :]
    sine_part = jnp.sin(angles)[..., None, :]
    leading = vectors[..., :half_width]
    trailing = vectors[..., half_width:]
    return jnp.concatenate(
        [leading * cosine - trailing * sine_part, trailing * cosine + leading * sine_part], axis=-1
    )


def attend(queries, key_rows, value_rows, key_places, key_valid, query_places):
    scores = jnp.einsum(
        "nhe,mhe->hnm", queries, key_rows, preferred_element_type=jnp.float32
    ) * queries.shape[-1] ** (-0.5)
    distance = query_places[:, None] - key_places[None, :]
    allowed = (
        key_valid[None, :] & (distance >= 0) & ((distance < WINDOW) | (key_places[None, :] < SINKS))
    )
    scores = jnp.where(allowed[None], scores, -1e30)
    highest = jnp.max(scores, axis=-1, keepdims=True)
    weights = jnp.exp(scores - highest)
    shares = (weights / jnp.sum(weights, axis=-1, keepdims=True)).astype(jnp.bfloat16)
    return jnp.einsum(
        "hnm,mhe->nhe", shares, value_rows, preferred_element_type=jnp.float32
    ).astype(jnp.bfloat16)


def body(
    hidden,
    cached_lengths,
    request_order,
    cache_keys,
    cache_values,
    attn_gain,
    w_qkv,
    w_out,
    moe_gain,
    expert_ids,
    gate_weights,
    w_in,
    w_down,
):
    tok_rows, model_width = hidden.shape
    heads_here = w_qkv.shape[1]
    head_width = w_qkv.shape[2] // 3
    normed = rms_scale(hidden, attn_gain).astype(jnp.bfloat16)
    qkv_matrix = w_qkv.reshape(model_width, heads_here * 3 * head_width)
    projected = jnp.dot(
        lax.all_gather(normed, "col", axis=0, tiled=True),
        qkv_matrix,
        preferred_element_type=jnp.float32,
    )
    new_rows = projected.shape[0]
    projected = projected.reshape(new_rows, heads_here, 3, head_width)
    row_index = lax.axis_index("row")
    places = jnp.arange(request_order.shape[0], dtype=jnp.int32)
    request = jnp.sum(jnp.where(places == row_index, request_order, 0))
    length = jnp.sum(jnp.where(places == request, cached_lengths, 0))
    query_pos = length + jnp.arange(new_rows, dtype=jnp.int32)
    queries = rotate(projected[:, :, 0], query_pos).astype(jnp.bfloat16)
    fresh_keys = rotate(projected[:, :, 1], query_pos).astype(jnp.bfloat16)
    fresh_values = projected[:, :, 2].astype(jnp.bfloat16)
    cache_rows = cache_keys.shape[1]
    cache_places = jnp.arange(cache_rows, dtype=jnp.int32)
    keys_all = jnp.concatenate(
        [cache_keys[0].reshape(cache_rows, heads_here, head_width), fresh_keys], axis=0
    )
    values_all = jnp.concatenate(
        [cache_values[0].reshape(cache_rows, heads_here, head_width), fresh_values], axis=0
    )
    key_places = jnp.concatenate([cache_places, query_pos])
    key_valid = jnp.concatenate([cache_places < length, jnp.ones((new_rows,), jnp.bool_)])
    block_rows = min(512, new_rows)
    query_blocks = queries.reshape(new_rows // block_rows, block_rows, heads_here, head_width)
    position_blocks = query_pos.reshape(new_rows // block_rows, block_rows)

    def one_block(operands):
        block_queries, block_places = operands
        return attend(block_queries, keys_all, values_all, key_places, key_valid, block_places)

    context = lax.map(one_block, (query_blocks, position_blocks)).reshape(
        new_rows, heads_here * head_width
    )
    attention = lax.psum_scatter(
        jnp.dot(context, w_out, preferred_element_type=jnp.float32).astype(jnp.bfloat16),
        "col",
        scatter_dimension=0,
        tiled=True,
    ).astype(jnp.float32)
    residual = hidden.astype(jnp.float32) + attention
    moe_in = rms_scale(residual, moe_gain).astype(jnp.bfloat16)
    top_count = expert_ids.shape[1]
    flat_ids = expert_ids.reshape(-1)
    onehot = (flat_ids[:, None] == jnp.arange(EXPERTS, dtype=jnp.int32)[None, :]).astype(jnp.int32)
    slot_rank = jnp.sum((jnp.cumsum(onehot, axis=0) - onehot) * onehot, axis=1)
    slot_index = flat_ids * CAP + slot_rank
    owners = jnp.arange(flat_ids.shape[0], dtype=jnp.int32) // top_count
    slot_table = jnp.full((EXPERTS * CAP,), tok_rows, jnp.int32).at[slot_index].set(owners)
    padded = jnp.concatenate([moe_in, jnp.zeros((1, model_width), jnp.bfloat16)], axis=0)
    routed_rows = padded[slot_table]
    row_count = lax.axis_size("row")
    col_count = lax.axis_size("col")
    device_count = row_count * col_count
    per_device = w_in.shape[0]
    half_units = w_down.shape[1]
    outgoing = routed_rows.reshape(EXPERTS, 1, CAP, model_width)
    outgoing = jnp.broadcast_to(outgoing, (EXPERTS, 2, CAP, model_width))
    sending = outgoing.reshape(device_count, per_device, CAP, model_width)
    both_parts = jnp.einsum(
        "shcd,hdf->shcf",
        lax.all_to_all(sending, ("row", "col"), split_axis=0, concat_axis=0, tiled=True),
        w_in,
        preferred_element_type=jnp.float32,
    )
    activated = (jax.nn.silu(both_parts[..., :half_units]) * both_parts[..., half_units:]).astype(
        jnp.bfloat16
    )
    results = jnp.einsum("shcf,hfd->shcd", activated, w_down, preferred_element_type=jnp.float32)
    returned = lax.all_to_all(
        results.astype(jnp.bfloat16), ("row", "col"), split_axis=0, concat_axis=0, tiled=True
    ).astype(results.dtype)
    flat_returned = returned.reshape(EXPERTS * 2 * CAP, model_width)
    half_ids = jnp.arange(2, dtype=jnp.int32)
    gather_index = (flat_ids[:, None] * 2 + half_ids[None, :]) * CAP + slot_rank[:, None]
    picked = flat_returned[gather_index.reshape(-1)].reshape(tok_rows, top_count, 2, model_width)
    part_rows = (picked[:, :, 0] + picked[:, :, 1]).astype(jnp.bfloat16)
    expert_sum = jnp.einsum(
        "tk,tkd->td", gate_weights, part_rows, preferred_element_type=jnp.float32
    )
    new_hidden = (residual + expert_sum).astype(jnp.bfloat16)
    new_keys = fresh_keys.reshape(new_rows, heads_here * head_width)
    new_values = fresh_values.reshape(new_rows, heads_here * head_width)
    return (new_hidden, new_keys, new_values)


def solution(mesh):
    in_specs = (
        P(("row", "col"), None),
        P(),
        P(),
        P("row", None, "col"),
        P("row", None, "col"),
        P(),
        P(None, "col", None),
        P("col", None),
        P(),
        P(("row", "col"), None),
        P(("row", "col"), None),
        P(("row", "col"), None, None),
        P(("row", "col"), None, None),
    )
    out_specs = (P(("row", "col"), None), P("row", "col"), P("row", "col"))
    return jax.shard_map(body, mesh=mesh, in_specs=in_specs, out_specs=out_specs, check_vma=False)
```

profile of v0, /device:TPU:0, one launch (start us, length us, event | category | flops | bytes accessed | tf_op | source)
XLA Modules:
  0.0 759.5 jit_solution(14790934212152108399)
XLA Ops:
  7.2 1.3 fusion.38
  9.2 2.0 fusion.40
  11.4 2.9 copy.47
  14.3 4.1 copy.48
  18.4 4.3 copy.75
  22.7 4.7 copy.43
  28.0 1.4 fusion.58
  31.5 1.8 multiply_cosine_fusion
  33.3 17.6 %all-gather.2.cloned.1.call-done = bf16[1024,2048]{1,0:T(8,128)(2,1)} async-done(((bf16[128,2048]{1,0:T(8,128)(2,1)}), bf16[1024,2048]{1,0:T(8,128)(2,1)}) %all-gather.2.cloned.1.call-update) | async-done | bytes 4194320 | tf_op jit(solution)/shard_map/all_gather | solution.py:71
  50.9 6.2 fusion.31
  57.2 1.6 copy-done.6
  58.7 1.5 slice_bitcast_fusion
  60.2 1.7 pad_maximum_fusion.1
  61.9 4.4 copy.50
  66.3 2.2 multiply_subtract_fusion
  68.5 2.2 subtract_convert_fusion
  77.0 1.7 pad_maximum_fusion
  78.7 4.4 copy.49
  83.1 1.5 pad_maximum_fusion.2
  84.6 102.0 %while.10 = (s32[]{:T(128)}, bf16[2,512,2,128]{3,2,1,0:T(2,128)(2,1)}, pred[5120]{0:T(1024)(128)(4,1)S(1)}, s32[2,512]{1,0:T(2,128)S(1)}, s32[5120]{0:T(1024)S(1...) while((s32[]{:T(128)}, ...), condition=%wide.region_6.7_spmd, body=%wide.region_3.6_spmd.sunk | while | flops 2742167552 | bytes 99685544 | solution.py:103
  85.1 3.6 fusion.78
  88.7 10.3 %fusion.77 = f32[2,512,5120]{2,1,0:T(8,128)} fusion(bf16[5120,2,128]{2,0,1:T(8,128)(2,1)} %get-tuple-element.178, bf16[2,512,2,128]{3,1,2,0:T(8,128)(2,1)S(1)} %get-tuple-element.177, s32[]{:T(128)S(6)} %copy.103), kind=kOutput, calls=%fused_computation.20.clone.1 | convolution fusion | flops 1342177280 | bytes 23855108 | tf_op jit(solution)/shard_map/while/body/eval_jaxpr/nhe,mhe->hnm/dot_general | solution.py:34
  99.1 25.0 %fusion.79 = (f32[2,512]{1,0:T(2,128)S(1)}, f32[2,512,5120]{2,1,0:T(8,128)}) fusion(f32[2,512,5120]{2,1,0:T(8,128)} %fusion.77, pred[512,5120]{1,0:T(8,128)(4,1)S(1)} %fusion.78), kind=kOutput, calls=%fused_computation.113.clone.1 | output fusion | flops 31462400 | bytes 44568576 | tf_op jit(solution)/shard_map/while/body/eval_jaxpr/sub | solution.py:43
  124.1 10.7 %fusion.80 = bf16[1,512,2,128]{3,1,2,0:T(8,128)(2,1)S(1)} fusion(bf16[5120,2,128]{2,0,1:T(8,128)(2,1)} %get-tuple-element.179, f32[2,512,5120]{2,1,0:T(8,128)} %get-tuple-element.152, f32[2,512]{1,0:T(2,128)S(1)} %get-tuple-element.153), kind=kOutput, calls=%fused_computation.18.clone.1 | convolution fusion | flops 1352794112 | bytes 23859200 | tf_op jit(solution)/shard_map/while/body/eval_jaxpr/hnm,mhe->nhe/dot_general | solution.py:45
  135.9 3.6 fusion.78
  139.5 10.3 %fusion.77 = f32[2,512,5120]{2,1,0:T(8,128)} fusion(bf16[5120,2,128]{2,0,1:T(8,128)(2,1)} %get-tuple-element.178, bf16[2,512,2,128]{3,1,2,0:T(8,128)(2,1)S(1)} %get-tuple-element.177, s32[]{:T(128)S(6)} %copy.103), kind=kOutput, calls=%fused_computation.20.clone.1 | convolution fusion | flops 1342177280 | bytes 23855108 | tf_op jit(solution)/shard_map/while/body/eval_jaxpr/nhe,mhe->hnm/dot_general | solution.py:34
  149.8 25.0 %fusion.79 = (f32[2,512]{1,0:T(2,128)S(1)}, f32[2,512,5120]{2,1,0:T(8,128)}) fusion(f32[2,512,5120]{2,1,0:T(8,128)} %fusion.77, pred[512,5120]{1,0:T(8,128)(4,1)S(1)} %fusion.78), kind=kOutput, calls=%fused_computation.113.clone.1 | output fusion | flops 31462400 | bytes 44568576 | tf_op jit(solution)/shard_map/while/body/eval_jaxpr/sub | solution.py:43
  174.8 10.7 %fusion.80 = bf16[1,512,2,128]{3,1,2,0:T(8,128)(2,1)S(1)} fusion(bf16[5120,2,128]{2,0,1:T(8,128)(2,1)} %get-tuple-element.179, f32[2,512,5120]{2,1,0:T(8,128)} %get-tuple-element.152, f32[2,512]{1,0:T(2,128)S(1)} %get-tuple-element.153), kind=kOutput, calls=%fused_computation.18.clone.1 | convolution fusion | flops 1352794112 | bytes 23859200 | tf_op jit(solution)/shard_map/while/body/eval_jaxpr/hnm,mhe->nhe/dot_general | solution.py:45
  186.6 4.3 convolution_convert_fusion
  191.6 1.8 reduce-window.6
  193.9 3.6 scatter_custom_fusion
  197.5 44.9 %reduce-scatter.2.cloned.1.call-done = bf16[128,2048]{1,0:T(8,128)(2,1)} async-done(((bf16[1024,2048]{1,0:T(8,128)(2,1)}), bf16[128,2048]{1,0:T(8,128)(2,1)}) %reduce-scatter.2.cloned.1.call-update) | async-done | bytes 524304 | tf_op jit(solution)/shard_map/reduce_scatter | solution.py:106
  242.4 1.3 multiply_reduce_fusion
  245.0 6.1 gather_fusion
  251.1 6.8 broadcast_in_dim.43
  257.8 188.2 %all_to_all.10 = bf16[32,4,16,2048]{3,2,1,0:T(8,128)(2,1)} all-to-all(bf16[32,4,16,2048]{3,2,1,0:T(8,128)(2,1)} %bitcast.105), channel_id=1, replica_groups=mesh['row'=4,'col'=8] {'row','col'}, dimensions={0} | all-to-all | bytes 16777216 | tf_op jit(solution)/shard_map/all_to_all | solution.py:133
  446.1 21.2 %fusion.22 = f32[32,4,16,1408]{3,2,0,1:T(8,128)} fusion(bf16[4,2048,1408]{2,1,0:T(8,128)(2,1)} %param.26, bf16[32,4,16,2048]{3,2,1,0:T(8,128)(2,1)} %all_to_all.10), kind=kOutput, calls=%fused_computation.35 | convolution fusion | flops 11811160064 | bytes 42991616 | tf_op jit(solution)/shard_map/shcd,hdf->shcf/dot_general | solution.py:131
  467.2 15.5 %convert_bitcast_fusion = bf16[32,4,16,2048]{3,2,0,1:T(8,128)(2,1)} fusion(bf16[4,704,2048]{2,1,0:T(8,128)(2,1)} %param.27, f32[32,4,16,1408]{3,2,0,1:T(8,128)} %fusion.22), kind=kOutput, calls=%fused_computation.34 | convolution fusion | flops 5918425088 | bytes 32505856 | tf_op jit(solution)/shard_map/shcf,hfd->shcd/dot_general | solution.py:140
  482.7 8.3 %copy.57 = bf16[32,4,16,2048]{3,2,1,0:T(8,128)(2,1)} copy(bf16[32,4,16,2048]{3,2,0,1:T(8,128)(2,1)} %convert_bitcast_fusion) | data formatting | bytes 16777216 | tf_op jit(solution)/shard_map/convert_element_type | solution.py:142
  491.0 4.0 all-to-all-start.1
  495.7 1.3 slice.86
  499.0 182.0 %all-to-all-done.1 = bf16[32,4,16,2048]{3,2,1,0:T(8,128)(2,1)} async-done(((bf16[32,4,16,2048]{3,2,1,0:T(8,128)(2,1)}), bf16[32,4,16,2048]{3,2,1,0:T(8,128)(2,1)}, u32[]{:S(2)}, u32[]{:S(2)}) %all-to-all-start.1) | async-done | bytes 8388640 | tf_op jit(solution)/shard_map/all_to_all | solution.py:141
  681.0 11.2 %bitcast_convert_fusion = f32[2048,2048]{1,0:T(8,128)} fusion(bf16[32,4,16,2048]{3,2,1,0:T(8,128)(2,1)} %all-to-all-done.1), kind=kLoop, calls=%fused_computation.32 | loop fusion | flops 4194304 | bytes 25165824 | tf_op jit(solution)/shard_map/reshape | solution.py:144
  692.3 18.3 %gather_fusion.1 = f32[1536,2048]{1,0:T(8,128)} fusion(f32[2048,2048]{1,0:T(8,128)} %bitcast_convert_fusion, s32[2048]{0:T(1024)S(1)} %pad_clamp_fusion), kind=kCustom, calls=%fused_computation.1 | custom fusion | bytes 25171968 | tf_op jit(solution)/shard_map/gather | solution.py:147
  710.5 15.3 %reshape.296 = f32[128,6,2,2048]{3,2,1,0:T(2,128)} reshape(f32[1536,2048]{1,0:T(8,128)} %gather_fusion.1) | data formatting | bytes 25165824 | tf_op jit(solution)/shard_map/reshape | solution.py:147
  725.8 15.6 %fusion.61 = (f32[128,6,1,2048]{3,2,1,0:T(1,128)S(1)}, f32[128,6,1,2048]{3,2,1,0:T(1,128)S(1)}) fusion(f32[128,6,2,2048]{3,2,1,0:T(2,128)} %reshape.296), kind=kLoop, calls=%fused_computation.114 | loop fusion | bytes 25165824 | tf_op jit(solution)/shard_map/slice | solution.py:148
  741.4 7.2 fusion.35
  748.6 2.6 fusion.33
  (84 shorter events, 18.5 us)
Async XLA Ops:
  7.2 179.4 %copy-start = (bf16[256,2048]{1,0:T(8,128)(2,1)S(1)}, bf16[256,2048]{1,0:T(8,128)(2,1)}, u32[]{:S(2)}) copy-start(bf16[256,2048]{1,0:T(8,128)(2,1)} %param.22) | copy-start | bytes 3145732
  7.2 43.7 %all-gather.2.cloned.1.call-start = ((), (), s32[]{:S(2)}) async-start(), calls=%async_computation.3 | async-start | bytes 4718592 | tf_op jit(solution)/shard_map/all_gather | solution.py:71
  11.3 231.1 %reduce-scatter.2.cloned.1.call-start = ((), (), s32[]{:S(2)}) async-start(), calls=%async_computation.4 | async-start | bytes 4718592 | tf_op jit(solution)/shard_map/reduce_scatter | solution.py:106
  18.4 9.0 %copy-start.12 = (s32[4]{0:T(128)S(1)}, s32[4]{0:T(128)}, u32[]{:S(2)}) copy-start(s32[4]{0:T(128)} %param.17) | copy-start | bytes 52
  18.4 9.6 %copy-start.13 = (s32[4]{0:T(128)S(1)}, s32[4]{0:T(128)}, u32[]{:S(2)}) copy-start(s32[4]{0:T(128)} %param.16) | copy-start | bytes 52
  57.1 1.7 copy-start.6
  57.1 3.1 copy-start.2
  76.2 0.8 copy-start.3
  124.1 10.7 %copy-start.7 = (bf16[2,512,2,128]{3,2,1,0:T(2,128)(2,1)S(1)}, bf16[2,512,2,128]{3,2,1,0:T(2,128)(2,1)}, u32[]{:S(2)}) copy-start(bf16[2,512,2,128]{3,2,1,0:T(2,128)(2,1)} %get-tuple-element.164) | copy-start | bytes 1572868 | tf_op jit(solution)/shard_map/while
  135.1 0.8 copy-start.8
  174.8 10.7 %copy-start.7 = (bf16[2,512,2,128]{3,2,1,0:T(2,128)(2,1)S(1)}, bf16[2,512,2,128]{3,2,1,0:T(2,128)(2,1)}, u32[]{:S(2)}) copy-start(bf16[2,512,2,128]{3,2,1,0:T(2,128)(2,1)} %get-tuple-element.164) | copy-start | bytes 1572868 | tf_op jit(solution)/shard_map/while
  185.8 0.8 copy-start.8
  186.6 4.3 copy-start.9
  186.6 4.7 copy-start.10
  186.6 55.8 %copy-start.1 = (bf16[128,2048]{1,0:T(8,128)(2,1)S(1)}, bf16[128,2048]{1,0:T(8,128)(2,1)}, u32[]{:S(2)}) copy-start(bf16[128,2048]{1,0:T(8,128)(2,1)} %param.15) | copy-start | bytes 1572868
  491.0 4.0 copy-start.11
  491.0 7.0 copy-start.4
  491.0 190.0 %all-to-all-start.1 = ((bf16[32,4,16,2048]{3,2,1,0:T(8,128)(2,1)}), bf16[32,4,16,2048]{3,2,1,0:T(8,128)(2,1)}, u32[]{:S(2)}, u32[]{:S(2)}) async-start(bf16[32,4,16,2048]{3,2,1,0:T(8,128)(2,1)} %copy.57), calls=%async_computation.2 | async-start | bytes 16777216 | tf_op jit(solution)/shard_map/all_to_all | solution.py:141
  748.6 2.6 copy-start.5
Sparse Core Ops, SparseCore 0:
  11.4 39.4 all-gather.1
  191.0 51.3 reduce-scatter.1
where the time goes:
time: 767 us; the launch traced here: 759 us
  waiting for transfers between devices  245 us (32%)
  blocking collectives  188 us (25%)
  local copies, waits for them, and re-layouts  114 us (15%)
  other arithmetic  102 us (13%)
  matrix products  91.8 us (12%)
  between operations  14.6 us (2%)
    all_to_all x1, blocking collectives, body(): lax.all_to_all(sending, ('row', 'col'), split_axis=0, concat_axis=0, tile...  188 us
    all_to_all x1, waiting for transfers between devices, body(): lax.all_to_all(results.astype(jnp.bfloat16), ('row', 'col'), split_axis=0...  182 us
    sub x2, other arithmetic, attend(): weights = jnp.exp(scores - highest)  49.9 us
    reduce_scatter x1, waiting for transfers between devices, body(): lax.psum_scatter(jnp.dot(context, w_out, preferred_element_type=jnp.float...  44.9 us
    dot_general x2, matrix products, attend(): jnp.einsum('hnm,mhe->nhe', shares, value_rows, preferred_element_type=jnp...  21.4 us
    dot_general x1, matrix products, body(): jnp.einsum('shcd,hdf->shcf', lax.all_to_all(sending, ('row', 'col'), spli...  21.2 us
    dot_general x2, matrix products, attend(): jnp.einsum('nhe,mhe->hnm', queries, key_rows, preferred_element_type=jnp....  20.7 us
    gather x1, local copies, waits for them, and re-layouts, body(): flat_returned[gather_index.reshape(-1)]  18.3 us
  transfers between devices with their start and end apart: 3, of which 3 were waited for; matrix products, arithmetic and copies ran while one was open for 4% of the time, Pallas kernels for 0%

commit v1 on v0

--- a/solution.py
+++ b/solution.py
@@ -67,11 +67,23 @@
     head_width = w_qkv.shape[2] // 3
     normed = rms_scale(hidden, attn_gain).astype(jnp.bfloat16)
     qkv_matrix = w_qkv.reshape(model_width, heads_here * 3 * head_width)
-    projected = jnp.dot(
-        lax.all_gather(normed, "col", axis=0, tiled=True),
-        qkv_matrix,
-        preferred_element_type=jnp.float32,
-    )
+
+    def form_pairs_all(load):
+        before, spare = (lax.axis_size("col"), lax.axis_index("col"))
+        then, z_new = (load, 1)
+        while z_new < before:
+            low = lax.ppermute(
+                then,
+                axis_name="col",
+                perm=list(map(lambda hop_no: (hop_no, hop_no ^ z_new), range(before))),
+            )
+            reached = jnp.concatenate([then, low], 0)
+            tile_out = jnp.concatenate([low, then], axis=0)
+            then = jnp.where(spare & z_new == 0, reached, tile_out)
+            z_new = 2 * z_new
+        return then
+
+    projected = jnp.dot(form_pairs_all(normed), qkv_matrix, preferred_element_type=jnp.float32)
     new_rows = projected.shape[0]
     projected = projected.reshape(new_rows, heads_here, 3, head_width)
     row_index = lax.axis_index("row")

time: 767 us -> 808 us (1.053)
  waiting for transfers between devices: 245 us -> 277 us
    ppermute x0 -> x3, waiting for transfers between devices: none -> 48.9 us  [form_pairs_all(): lax.ppermute(then, axis_name='col', perm=list(map(lambda hop_no: (hop_no,...]
    all_gather x1 -> x0, waiting for transfers between devices: 17.6 us -> none  [body(): lax.all_gather(normed, 'col', axis=0, tiled=True)]
  transfers between devices with their start and end apart: 3 -> 5, of which waited for: 3 -> 5; matrix products, arithmetic and copies ran while one was open for 4% -> 4% of each run, Pallas kernels for 0% -> 0%
where the time goes in v1:
time: 808 us; the launch traced here: 799 us
  waiting for transfers between devices  277 us (34%)
  blocking collectives  188 us (23%)
  local copies, waits for them, and re-layouts  114 us (14%)
  other arithmetic  102 us (13%)
  matrix products  93.5 us (12%)
  between operations  14.6 us (2%)
  starting transfers between devices  9.24 us (1%)
    all_to_all x1, blocking collectives, body(): lax.all_to_all(sending, ('row', 'col'), split_axis=0, concat_axis=0, tile...  188 us
    all_to_all x1, waiting for transfers between devices, body(): lax.all_to_all(results.astype(jnp.bfloat16), ('row', 'col'), split_axis=0...  182 us
    sub x2, other arithmetic, attend(): weights = jnp.exp(scores - highest)  49.9 us
    ppermute x3, waiting for transfers between devices, form_pairs_all(): lax.ppermute(then, axis_name='col', perm=list(map(lambda hop_no: (hop_no,...  48.9 us
    reduce_scatter x1, waiting for transfers between devices, body(): lax.psum_scatter(jnp.dot(context, w_out, preferred_element_type=jnp.float...  45.9 us
    dot_general x2, matrix products, attend(): jnp.einsum('hnm,mhe->nhe', shares, value_rows, preferred_element_type=jnp...  21.4 us
    dot_general x1, matrix products, body(): jnp.einsum('shcd,hdf->shcf', lax.all_to_all(sending, ('row', 'col'), spli...  21.2 us
    dot_general x2, matrix products, attend(): jnp.einsum('nhe,mhe->hnm', queries, key_rows, preferred_element_type=jnp....  20.7 us
  transfers between devices with their start and end apart: 5, of which 5 were waited for; matrix products, arithmetic and copies ran while one was open for 4% of the time, Pallas kernels for 0%

profile of v1, /device:TPU:0, one launch (start us, length us, event | category | flops | bytes accessed | tf_op | source)
XLA Modules:
  0.0 799.1 jit_solution(9004725853105368397)
XLA Ops:
  7.2 1.3 fusion.45
  11.0 1.5 collective-permute-done
  12.8 2.9 collective-permute-start.1
  15.7 23.5 %collective-permute-done.1 = bf16[256,2048]{1,0:T(8,128)(2,1)S(1)} collective-permute-done((bf16[256,2048]{1,0:T(8,128)(2,1)S(1)}, bf16[256,2048]{1,0:T(8,128)(2,1)S(1)}, u32[]{:S(2)}, u32[]{:S(2)}) %collective-permute-start.1) | collective-permute-done | bytes 1048608 | tf_op jit(solution)/shard_map/ppermute | solution.py:75
  39.2 2.4 maximum_select_fusion.1
  41.6 1.8 collective-permute-start.2
  43.3 2.9 copy.47
  46.3 4.2 copy.48
  50.4 4.3 copy.75
  54.7 4.8 copy.43
  63.4 1.8 multiply_cosine_fusion
  65.1 23.9 %collective-permute-done.2 = bf16[512,2048]{1,0:T(8,128)(2,1)} collective-permute-done((bf16[512,2048]{1,0:T(8,128)(2,1)}, bf16[512,2048]{1,0:T(8,128)(2,1)}, u32[]{:S(2)}, u32[]{:S(2)}) %collective-permute-start.2) | collective-permute-done | bytes 2097184 | tf_op jit(solution)/shard_map/ppermute | solution.py:75
  89.0 7.9 fusion.32
  97.0 1.6 copy-done.6
  98.6 1.5 slice_bitcast_fusion
  100.0 1.7 pad_maximum_fusion.1
  101.8 4.4 copy.50
  106.1 2.2 multiply_subtract_fusion
  108.4 2.2 subtract_convert_fusion
  116.9 1.7 pad_maximum_fusion
  118.6 4.5 copy.49
  123.4 101.7 %while.10 = (s32[]{:T(128)}, bf16[2,512,2,128]{3,2,1,0:T(2,128)(2,1)}, pred[5120]{0:T(1024)(128)(4,1)S(1)}, s32[2,512]{1,0:T(2,128)S(1)}, s32[5120]{0:T(1024)S(1...) while((s32[]{:T(128)}, ...), condition=%wide.region_6.7_spmd, body=%wide.region_3.6_spmd.sunk | while | flops 2742167552 | bytes 99685544 | solution.py:115
  123.6 3.6 fusion.86
  127.2 10.3 %fusion.85 = f32[2,512,5120]{2,1,0:T(8,128)} fusion(bf16[5120,2,128]{2,0,1:T(8,128)(2,1)} %get-tuple-element.178, bf16[2,512,2,128]{3,1,2,0:T(8,128)(2,1)S(1)} %get-tuple-element.177, s32[]{:T(128)S(6)} %copy.103), kind=kOutput, calls=%fused_computation.20.clone.1 | convolution fusion | flops 1342177280 | bytes 23855108 | tf_op jit(solution)/shard_map/while/body/eval_jaxpr/nhe,mhe->hnm/dot_general | solution.py:34
  137.6 25.0 %fusion.87 = (f32[2,512]{1,0:T(2,128)S(1)}, f32[2,512,5120]{2,1,0:T(8,128)}) fusion(f32[2,512,5120]{2,1,0:T(8,128)} %fusion.85, pred[512,5120]{1,0:T(8,128)(4,1)S(1)} %fusion.86), kind=kOutput, calls=%fused_computation.123.clone.1 | output fusion | flops 31462400 | bytes 44568576 | tf_op jit(solution)/shard_map/while/body/eval_jaxpr/sub | solution.py:43
  162.5 10.7 %fusion.88 = bf16[1,512,2,128]{3,1,2,0:T(8,128)(2,1)S(1)} fusion(bf16[5120,2,128]{2,0,1:T(8,128)(2,1)} %get-tuple-element.179, f32[2,512,5120]{2,1,0:T(8,128)} %get-tuple-element.152, f32[2,512]{1,0:T(2,128)S(1)} %get-tuple-element.153), kind=kOutput, calls=%fused_computation.18.clone.1 | convolution fusion | flops 1352794112 | bytes 23859200 | tf_op jit(solution)/shard_map/while/body/eval_jaxpr/hnm,mhe->nhe/dot_general | solution.py:45
  174.3 3.6 fusion.86
  177.9 10.3 %fusion.85 = f32[2,512,5120]{2,1,0:T(8,128)} fusion(bf16[5120,2,128]{2,0,1:T(8,128)(2,1)} %get-tuple-element.178, bf16[2,512,2,128]{3,1,2,0:T(8,128)(2,1)S(1)} %get-tuple-element.177, s32[]{:T(128)S(6)} %copy.103), kind=kOutput, calls=%fused_computation.20.clone.1 | convolution fusion | flops 1342177280 | bytes 23855108 | tf_op jit(solution)/shard_map/while/body/eval_jaxpr/nhe,mhe->hnm/dot_general | solution.py:34
  188.3 25.0 %fusion.87 = (f32[2,512]{1,0:T(2,128)S(1)}, f32[2,512,5120]{2,1,0:T(8,128)}) fusion(f32[2,512,5120]{2,1,0:T(8,128)} %fusion.85, pred[512,5120]{1,0:T(8,128)(4,1)S(1)} %fusion.86), kind=kOutput, calls=%fused_computation.123.clone.1 | output fusion | flops 31462400 | bytes 44568576 | tf_op jit(solution)/shard_map/while/body/eval_jaxpr/sub | solution.py:43
  213.3 10.7 %fusion.88 = bf16[1,512,2,128]{3,1,2,0:T(8,128)(2,1)S(1)} fusion(bf16[5120,2,128]{2,0,1:T(8,128)(2,1)} %get-tuple-element.179, f32[2,512,5120]{2,1,0:T(8,128)} %get-tuple-element.152, f32[2,512]{1,0:T(2,128)S(1)} %get-tuple-element.153), kind=kOutput, calls=%fused_computation.18.clone.1 | convolution fusion | flops 1352794112 | bytes 23859200 | tf_op jit(solution)/shard_map/while/body/eval_jaxpr/hnm,mhe->nhe/dot_general | solution.py:45
  225.1 4.3 convolution_convert_fusion
  230.1 1.8 reduce-window.6
  232.4 3.8 scatter_custom_fusion
  236.2 45.9 %reduce-scatter.2.cloned.1.call-done = bf16[128,2048]{1,0:T(8,128)(2,1)} async-done(((bf16[1024,2048]{1,0:T(8,128)(2,1)}), bf16[128,2048]{1,0:T(8,128)(2,1)}) %reduce-scatter.2.cloned.1.call-update) | async-done | bytes 524304 | tf_op jit(solution)/shard_map/reduce_scatter | solution.py:118
  284.7 6.1 gather_fusion
  290.7 6.8 broadcast_in_dim.43
  297.5 188.2 %all_to_all.10 = bf16[32,4,16,2048]{3,2,1,0:T(8,128)(2,1)} all-to-all(bf16[32,4,16,2048]{3,2,1,0:T(8,128)(2,1)} %bitcast.105), channel_id=1, replica_groups=mesh['row'=4,'col'=8] {'row','col'}, dimensions={0} | all-to-all | bytes 16777216 | tf_op jit(solution)/shard_map/all_to_all | solution.py:145
  485.7 21.2 %fusion.22 = f32[32,4,16,1408]{3,2,0,1:T(8,128)} fusion(bf16[4,2048,1408]{2,1,0:T(8,128)(2,1)} %param.26, bf16[32,4,16,2048]{3,2,1,0:T(8,128)(2,1)} %all_to_all.10), kind=kOutput, calls=%fused_computation.35 | convolution fusion | flops 11811160064 | bytes 42991616 | tf_op jit(solution)/shard_map/shcd,hdf->shcf/dot_general | solution.py:143
  506.9 15.5 %convert_bitcast_fusion = bf16[32,4,16,2048]{3,2,0,1:T(8,128)(2,1)} fusion(bf16[4,704,2048]{2,1,0:T(8,128)(2,1)} %param.27, f32[32,4,16,1408]{3,2,0,1:T(8,128)} %fusion.22), kind=kOutput, calls=%fused_computation.34 | convolution fusion | flops 5918425088 | bytes 32505856 | tf_op jit(solution)/shard_map/shcf,hfd->shcd/dot_general | solution.py:152
  522.4 8.3 %copy.57 = bf16[32,4,16,2048]{3,2,1,0:T(8,128)(2,1)} copy(bf16[32,4,16,2048]{3,2,0,1:T(8,128)(2,1)} %convert_bitcast_fusion) | data formatting | bytes 16777216 | tf_op jit(solution)/shard_map/convert_element_type | solution.py:154
  530.6 4.0 all-to-all-start.1
  538.7 182.0 %all-to-all-done.1 = bf16[32,4,16,2048]{3,2,1,0:T(8,128)(2,1)} async-done(((bf16[32,4,16,2048]{3,2,1,0:T(8,128)(2,1)}), bf16[32,4,16,2048]{3,2,1,0:T(8,128)(2,1)}, u32[]{:S(2)}, u32[]{:S(2)}) %all-to-all-start.1) | async-done | bytes 8388640 | tf_op jit(solution)/shard_map/all_to_all | solution.py:153
  720.7 11.2 %bitcast_convert_fusion = f32[2048,2048]{1,0:T(8,128)} fusion(bf16[32,4,16,2048]{3,2,1,0:T(8,128)(2,1)} %all-to-all-done.1), kind=kLoop, calls=%fused_computation.32 | loop fusion | flops 4194304 | bytes 25165824 | tf_op jit(solution)/shard_map/reshape | solution.py:156
  731.9 18.3 %gather_fusion.1 = f32[1536,2048]{1,0:T(8,128)} fusion(f32[2048,2048]{1,0:T(8,128)} %bitcast_convert_fusion, s32[2048]{0:T(1024)S(1)} %pad_clamp_fusion), kind=kCustom, calls=%fused_computation.1 | custom fusion | bytes 25171968 | tf_op jit(solution)/shard_map/gather | solution.py:159
  750.2 15.3 %reshape.296 = f32[128,6,2,2048]{3,2,1,0:T(2,128)} reshape(f32[1536,2048]{1,0:T(8,128)} %gather_fusion.1) | data formatting | bytes 25165824 | tf_op jit(solution)/shard_map/reshape | solution.py:159
  765.5 15.6 %fusion.69 = (f32[128,6,1,2048]{3,2,1,0:T(1,128)S(1)}, f32[128,6,1,2048]{3,2,1,0:T(1,128)S(1)}) fusion(f32[128,6,2,2048]{3,2,1,0:T(2,128)} %reshape.296), kind=kLoop, calls=%fused_computation.124 | loop fusion | bytes 25165824 | tf_op jit(solution)/shard_map/slice | solution.py:160
  781.0 7.2 fusion.42
  788.2 2.6 fusion.39
  (93 shorter events, 24.4 us)
Async XLA Ops:
  7.2 217.9 %copy-start = (bf16[256,2048]{1,0:T(8,128)(2,1)S(1)}, bf16[256,2048]{1,0:T(8,128)(2,1)}, u32[]{:S(2)}) copy-start(bf16[256,2048]{1,0:T(8,128)(2,1)} %param.22) | copy-start | bytes 3145732
  7.2 274.8 %reduce-scatter.2.cloned.1.call-start = ((), (), s32[]{:S(2)}) async-start(), calls=%async_computation.3 | async-start | bytes 4718592 | tf_op jit(solution)/shard_map/reduce_scatter | solution.py:118
  10.5 2.1 collective-permute-start
  12.8 26.4 %collective-permute-start.1 = (bf16[256,2048]{1,0:T(8,128)(2,1)S(1)}, bf16[256,2048]{1,0:T(8,128)(2,1)S(1)}, u32[]{:S(2)}, u32[]{:S(2)}) collective-permute-start(bf16[256,2048]{1,0:T(8,128)(2,1)S(1)} %maximum_select_fusion.2), channel_id=1, source_target_pairs={{0,2},{1,3},{2,0},{3,1},{4,6},{5,7},{6,4},{7,5},{8,10},{9,11},{10,... | collective-permute-start | bytes 3145736 | tf_op jit(solution)/shard_map/ppermute | solution.py:75
  41.6 47.5 %collective-permute-start.2 = (bf16[512,2048]{1,0:T(8,128)(2,1)}, bf16[512,2048]{1,0:T(8,128)(2,1)}, u32[]{:S(2)}, u32[]{:S(2)}) collective-permute-start(bf16[512,2048]{1,0:T(8,128)(2,1)} %maximum_select_fusion.1), channel_id=1, source_target_pairs={{0,4},{1,5},{2,6},{3,7},{4,0},{5,1},{6,2},{7,3},{8,12},{9,13},{10,... | collective-permute-start | bytes 6291464 | tf_op jit(solution)/shard_map/ppermute | solution.py:75
  50.4 9.0 %copy-start.14 = (s32[4]{0:T(128)S(1)}, s32[4]{0:T(128)}, u32[]{:S(2)}) copy-start(s32[4]{0:T(128)} %param.17) | copy-start | bytes 52
  50.4 9.7 %copy-start.15 = (s32[4]{0:T(128)S(1)}, s32[4]{0:T(128)}, u32[]{:S(2)}) copy-start(s32[4]{0:T(128)} %param.16) | copy-start | bytes 52
  96.9 1.7 copy-start.6
  96.9 3.1 copy-start.2
  116.1 0.8 copy-start.3
  118.6 4.5 copy-start.7
  118.6 4.5 copy-start.8
  162.5 10.7 %copy-start.9 = (bf16[2,512,2,128]{3,2,1,0:T(2,128)(2,1)S(1)}, bf16[2,512,2,128]{3,2,1,0:T(2,128)(2,1)}, u32[]{:S(2)}) copy-start(bf16[2,512,2,128]{3,2,1,0:T(2,128)(2,1)} %get-tuple-element.164) | copy-start | bytes 1572868 | tf_op jit(solution)/shard_map/while
  173.5 0.8 copy-start.10
  213.3 10.7 %copy-start.9 = (bf16[2,512,2,128]{3,2,1,0:T(2,128)(2,1)S(1)}, bf16[2,512,2,128]{3,2,1,0:T(2,128)(2,1)}, u32[]{:S(2)}) copy-start(bf16[2,512,2,128]{3,2,1,0:T(2,128)(2,1)} %get-tuple-element.164) | copy-start | bytes 1572868 | tf_op jit(solution)/shard_map/while
  224.3 0.8 copy-start.10
  225.1 4.3 copy-start.11
  225.1 4.7 copy-start.12
  225.1 57.0 %copy-start.1 = (bf16[128,2048]{1,0:T(8,128)(2,1)S(1)}, bf16[128,2048]{1,0:T(8,128)(2,1)}, u32[]{:S(2)}) copy-start(bf16[128,2048]{1,0:T(8,128)(2,1)} %param.15) | copy-start | bytes 1572868
  530.6 4.0 copy-start.13
  530.6 7.0 copy-start.4
  530.6 190.0 %all-to-all-start.1 = ((bf16[32,4,16,2048]{3,2,1,0:T(8,128)(2,1)}), bf16[32,4,16,2048]{3,2,1,0:T(8,128)(2,1)}, u32[]{:S(2)}, u32[]{:S(2)}) async-start(bf16[32,4,16,2048]{3,2,1,0:T(8,128)(2,1)} %copy.57), calls=%async_computation.2 | async-start | bytes 16777216 | tf_op jit(solution)/shard_map/all_to_all | solution.py:153
  788.2 2.6 copy-start.5
Sparse Core Ops, SparseCore 0:
  229.5 52.4 reduce-scatter.1
